TPU v7x, 32 devices: a whole 2x2x4 slice. The times are simulated.
32 devices in a mesh: groups: 2 (over x), space: 16 (over z, y, core).
Axes of the slice: x: 2, y: 2, z: 4, core: 2. Of those that a mesh axis runs over, the one named last changes fastest.
Arguments:
- lifted_field: float32 [64, 16, 128, 256], P('groups', 'space'), parts along dimension 0, may hold values from -6 to 6
- cotangent: bfloat16 [64, 16, 128, 256], P('groups', 'space'), parts along dimension 0, may hold values from -6 to 6
- spectral_weights: float32 [2, 32, 1024, 32, 32], P(None, None, 'space'), may hold values from -4 to 4
- point_weights: float32 [32, 32], replicated, may hold values from -1 to 1
- point_bias: float32 [32], replicated, may hold values from -3 to 3
Outputs:
- activated: bfloat16 [64, 16, 128, 256], P('groups', 'space'), parts along dimension 0
- grad_spectral: float32 [4, 32, 1024, 32, 32], P('groups', None, 'space'), parts along dimension 0
- grad_point: float32 [64, 32], P('groups'), parts along dimension 0
- grad_bias: float32 [64], P('groups'), parts along dimension 0
There are 2 independent parts, one for each index of `groups`. A program takes and returns all parts, laid end to end along the dimension named above; an argument that names none is the same for every part. Nothing has to cross between parts.
All inputs are finite; a program needn't handle non-finite values.
Results may differ from a plain program's by a relative error of at most 0.001.
Values sent between devices are 32-bit elements; how exact they have to be, the bound alone decides.
A program may use at most 192 MiB of HBM per device.

v0:
```python
import functools

import jax
import jax.numpy as jnp
import numpy as np
from jax import lax
from jax.experimental import pallas as pl
from jax.experimental.pallas import tpu as pltpu
from jax.sharding import PartitionSpec as P

MX = 32
MY = 32
MZ = 32
ROWS = 8
STEP = 16

HIGH = lax.Precision.HIGH
INV_SQRT_TWO = 0.7071067811865476
INV_SQRT_TWO_PI = 0.3989422804014327


def angles(positions, frequency, length):
    product = np.outer(np.asarray(positions), np.asarray(frequency)) % length
    phase = 2.0 * np.pi / length * product.astype(np.float64)
    return np.cos(phase), np.sin(phase)


def kept(count, length):
    index = np.arange(count)
    return np.where(index < count // 2, index, length - count + index)


def halves(table):
    table = np.asarray(table, np.float32)
    high = table.astype(jnp.bfloat16)
    low = (table - high.astype(np.float32)).astype(jnp.bfloat16)
    return jnp.asarray(high), jnp.asarray(low)


def split(value):
    high = value.astype(jnp.bfloat16)
    low = (value - high.astype(jnp.float32)).astype(jnp.bfloat16)
    return high, low


def dot3(a, b, dims=(((1,), (0,)), ((), ()))):
    one = functools.partial(
        lax.dot_general, dimension_numbers=dims, preferred_element_type=jnp.float32
    )
    return one(a[0], b[0]) + (one(a[0], b[1]) + one(a[1], b[0]))


def forward_tables(ny, nz):
    cos_z, sin_z = angles(np.arange(nz), np.arange(MZ), nz)
    table_z = np.concatenate([cos_z, -sin_z, -sin_z, -cos_z], axis=1)
    cos_y, sin_y = angles(np.arange(ny), kept(MY, ny), ny)
    table_y = np.concatenate([cos_y.T, sin_y.T], axis=0)
    return halves(table_z) + halves(table_y)


def inverse_tables(ny, nz, scale):
    cos_z, sin_z = angles(np.arange(nz), np.arange(MZ), nz)
    weight = np.where(np.arange(MZ) == 0, 1.0, 2.0)[:, None] * scale
    table = np.concatenate([cos_z.T * weight, -sin_z.T * weight], axis=0)
    blocks = np.kron(np.eye(4), table)
    cos_y, sin_y = angles(np.arange(ny), kept(MY, ny), ny)
    table_y = np.concatenate([cos_y, -sin_y], axis=1)
    return halves(blocks) + halves(table_y)


def finish_y(lines, ty, modes_ref):
    def one(c, carry):
        both = dot3(ty, split(lines[c]))
        turned = pltpu.roll(both[MY:], 2 * MZ, 1)
        modes_ref[c] = (both[:MY] + turned)[:, : 2 * MZ]
        return carry

    lax.fori_loop(0, lines.shape[0], one, 0, unroll=4)


def forward_kernel(x_ref, tzh, tzl, tyh, tyl, modes_ref, lines):
    step = pl.program_id(1)
    channels, rows, nz = x_ref.shape
    value = x_ref[...].reshape(channels * rows, nz)
    along = dot3(split(value), (tzh[...], tzl[...]))
    start = pl.multiple_of(step * rows, rows)
    lines[:, pl.ds(start, rows), :] = along.reshape(channels, rows, 4 * MZ)

    @pl.when(step == pl.num_programs(1) - 1)
    def _():
        finish_y(lines, (tyh[...], tyl[...]), modes_ref)


def whole(array):
    shape = array.shape
    return pl.BlockSpec(shape, lambda *_: (0,) * len(shape))


def field_spec(channels, nz):
    return pl.BlockSpec((channels, None, STEP, nz), lambda x, y: (0, x, y, 0))


def modes_spec(channels):
    return pl.BlockSpec((None, channels, MY, 2 * MZ), lambda x, y: (x, 0, 0, 0))


def forward_modes(field):
    channels, width, ny, nz = field.shape
    tables = forward_tables(ny, nz)
    return pl.pallas_call(
        forward_kernel,
        grid=(width, ny // STEP),
        out_shape=jax.ShapeDtypeStruct((width, channels, MY, 2 * MZ), jnp.float32),
        in_specs=[field_spec(channels, nz)] + [whole(t) for t in tables],
        out_specs=modes_spec(channels),
        scratch_shapes=[pltpu.VMEM((channels, ny, 4 * MZ), jnp.float32)],
        name="forward_modes",
    )(field, *tables)


def middle_kernel(
    m_ref, x_ref, cot_ref, wk_ref, bias_ref, bdh, bdl, iyh, iyl, tzh, tzl, tyh, tyl,
    act_ref, modes_ref, point_ref, lines, inverse, wh, wl, total,
):
    step = pl.program_id(1)
    channels, rows, nz = x_ref.shape
    quads = channels // 4
    width = 8 * MZ

    @pl.when(step == 0)
    def _():
        for part in range(0, m_ref.shape[1], 512):
            lanes = pl.ds(part, 512)
            inverse[:, lanes] = dot3((iyh[...], iyl[...]), split(m_ref[:, lanes]))
        high, low = split(wk_ref[...])
        wh[...] = high
        wl[...] = low
        total[...] = jnp.zeros_like(total)

    for half in range(rows // ROWS):
        start = pl.multiple_of(step * rows + half * ROWS, ROWS)
        stacked = jnp.concatenate(
            [inverse[pl.ds(start, ROWS), g * width : (g + 1) * width] for g in range(quads)], axis=0
        )
        spectral = dot3(split(stacked), (bdh[...], bdl[...]))
        spectral = jnp.concatenate(
            [
                spectral[g * ROWS : (g + 1) * ROWS, c * nz : (c + 1) * nz]
                for g in range(quads)
                for c in range(4)
            ],
            axis=0,
        )
        field = x_ref[:, half * ROWS : (half + 1) * ROWS, :].reshape(channels * ROWS, nz)
        field = split(field)
        before = spectral + dot3((wh[...], wl[...]), field) + bias_ref[...]
        normal = 0.5 * (1.0 + lax.erf(before * INV_SQRT_TWO))
        density = jnp.exp(-0.5 * before * before) * INV_SQRT_TWO_PI
        act_ref[:, half * ROWS : (half + 1) * ROWS, :] = (
            (before * normal).reshape(channels, ROWS, nz).astype(jnp.bfloat16)
        )
        cot = cot_ref[:, half * ROWS : (half + 1) * ROWS, :].astype(jnp.float32)
        slope = cot.reshape(channels * ROWS, nz) * (normal + before * density)
        slope = split(slope)
        total[...] += dot3(field, slope, (((1,), (1,)), ((), ())))
        along = dot3(slope, (tzh[...], tzl[...]))
        lines[:, pl.ds(start, ROWS), :] = along.reshape(channels, ROWS, 4 * MZ)

    @pl.when(step == pl.num_programs(1) - 1)
    def _():
        finish_y(lines, (tyh[...], tyl[...]), modes_ref)
        size = channels * ROWS
        row = lax.broadcasted_iota(jnp.int32, (size, size), 0) % ROWS
        column = lax.broadcasted_iota(jnp.int32, (size, size), 1) % ROWS
        diagonal = jnp.where(row == column, total[...], 0.0)
        point_ref[...] = jnp.sum(diagonal.reshape(channels, ROWS, size), axis=1)


def middle(grid_modes, field, cotangent, point_weights, point_bias, scale):
    channels, width, ny, nz = field.shape
    size = channels * ROWS
    tables = inverse_tables(ny, nz, scale) + forward_tables(ny, nz)
    eye = jnp.eye(ROWS, dtype=jnp.float32)
    wide = (point_weights.T[:, None, :, None] * eye[None, :, None, :]).reshape(size, size)
    bias = jnp.broadcast_to(jnp.repeat(point_bias, ROWS)[:, None], (size, nz))
    spec = field_spec(channels, nz)
    mixed_spec = pl.BlockSpec((None,) + grid_modes.shape[1:], lambda x, y: (x, 0, 0))
    return pl.pallas_call(
        middle_kernel,
        grid=(width, ny // STEP),
        out_shape=(
            jax.ShapeDtypeStruct(field.shape, jnp.bfloat16),
            jax.ShapeDtypeStruct((width, channels, MY, 2 * MZ), jnp.float32),
            jax.ShapeDtypeStruct((width, channels, size), jnp.float32),
        ),
        in_specs=[mixed_spec, spec, spec, whole(wide), whole(bias)] + [whole(t) for t in tables],
        out_specs=(
            spec,
            modes_spec(channels),
            pl.BlockSpec((None, channels, size), lambda x, y: (x, 0, 0)),
        ),
        scratch_shapes=[
            pltpu.VMEM((channels, ny, 4 * MZ), jnp.float32),
            pltpu.VMEM((ny, channels * 2 * MZ), jnp.float32),
            pltpu.VMEM((size, size), jnp.bfloat16),
            pltpu.VMEM((size, size), jnp.bfloat16),
            pltpu.VMEM((size, size), jnp.float32),
        ],
        name="middle",
    )(grid_modes, field, cotangent, wide, bias, *tables)


def gradient_kernel(s_ref, d_ref, out_ref):
    channels = s_ref.shape[1]
    d_real = d_ref[0]
    d_imag = d_ref[1]
    for i in range(channels):
        s_real = s_ref[0, i : i + 1, :]
        s_imag = s_ref[1, i : i + 1, :]
        out_ref[0, i] = s_real * d_real + s_imag * d_imag
        out_ref[1, i] = s_real * d_imag - s_imag * d_real


def weight_gradient(spectrum, slope_modes):
    _, kx, channels, modes = spectrum.shape
    spec = pl.BlockSpec((2, None, channels, modes), lambda k: (0, k, 0, 0))
    out = pl.pallas_call(
        gradient_kernel,
        grid=(kx,),
        out_shape=jax.ShapeDtypeStruct((2, kx, channels, channels, modes), jnp.float32),
        in_specs=[spec, spec],
        out_specs=pl.BlockSpec((2, None, channels, channels, modes), lambda k: (0, k, 0, 0, 0)),
        name="weight_gradient",
    )(spectrum, slope_modes)
    return out.transpose(0, 1, 4, 2, 3)


def x_table(length_x):
    return angles(np.arange(length_x), kept(MX, length_x), length_x)


def to_spectrum(modes, scale):
    width, channels = modes.shape[:2]
    lines = modes.reshape(width, channels, MY, 2, MZ).transpose(0, 3, 1, 2, 4)
    lines = lines.reshape(width, 2, channels, MY * MZ)
    lines = lax.all_to_all(lines, "space", split_axis=3, concat_axis=0, tiled=True)
    cos_x, sin_x = x_table(lines.shape[0])
    table = np.stack([np.stack([cos_x, -sin_x], 1), np.stack([sin_x, cos_x], 1)], 1)
    table = jnp.asarray((table * scale).astype(np.float32))
    return jnp.einsum("xrcm,xrqk->qkcm", lines, table, precision=HIGH)


def mix_modes(spectrum, weights):
    real, imag = spectrum[0], spectrum[1]
    out_real = jnp.einsum("kim,kmio->kom", real, weights[0], precision=HIGH) - jnp.einsum(
        "kim,kmio->kom", imag, weights[1], precision=HIGH
    )
    out_imag = jnp.einsum("kim,kmio->kom", real, weights[1], precision=HIGH) + jnp.einsum(
        "kim,kmio->kom", imag, weights[0], precision=HIGH
    )
    return jnp.stack([out_real, out_imag], axis=0)


def to_grid(mixed, length_x):
    channels = mixed.shape[2]
    cos_x, sin_x = x_table(length_x)
    table = np.stack([np.stack([cos_x, sin_x], 0), np.stack([-sin_x, cos_x], 0)], 0)
    table = jnp.asarray(table.astype(np.float32))
    lines = jnp.einsum("rkom,rqxk->xqom", mixed, table, precision=HIGH)
    lines = lax.all_to_all(lines, "space", split_axis=0, concat_axis=3, tiled=True)
    grid = lines.reshape(lines.shape[0], 2, channels, MY, MZ).transpose(0, 1, 3, 2, 4)
    real, imag = grid[:, 0], grid[:, 1]
    stacked = jnp.stack([jnp.stack([real, imag], 3), jnp.stack([imag, -real], 3)], 1)
    return stacked.reshape(lines.shape[0], 2 * MY, channels * 2 * MZ)


def body(lifted_field, cotangent, spectral_weights, point_weights, point_bias):
    devices = lax.axis_size("space")
    channels, width, ny, nz = lifted_field.shape
    length_x = width * devices
    scale = 1.0 / float(length_x * ny * nz) ** 0.5
    spectrum = to_spectrum(forward_modes(lifted_field), scale)
    grid_modes = to_grid(mix_modes(spectrum, spectral_weights), length_x)
    activated, slope_modes, wide_point = middle(
        grid_modes, lifted_field, cotangent, point_weights, point_bias, scale
    )
    local_point = jnp.sum(wide_point.reshape(width, channels, channels, ROWS), axis=(0, 3))
    local_bias = jnp.sum(slope_modes[:, :, 0, 0], axis=0)
    partial = jnp.concatenate([local_point, local_bias[None, :]], axis=0)
    copies = jnp.broadcast_to(partial[None], (devices,) + partial.shape)
    summed = jnp.sum(
        lax.all_to_all(copies, "space", split_axis=0, concat_axis=0, tiled=True), axis=0
    )
    slope_spectrum = to_spectrum(slope_modes, scale)
    local_modes = spectrum.shape[3]
    mode_ids = lax.axis_index("space") * local_modes + jnp.arange(local_modes, dtype=jnp.int32)
    weight_modes = jnp.where(mode_ids % MZ == 0, 1.0, 2.0).astype(jnp.float32)
    grad_spectral = weight_gradient(spectrum, slope_spectrum * weight_modes)
    return (activated, grad_spectral, summed[:-1] * scale, summed[-1] * scale)


def solution(mesh):
    placed = (
        P("groups", "space", None, None),
        P("groups", "space", None, None),
        P(None, None, "space", None, None),
        P(),
        P(),
    )
    return jax.shard_map(
        body,
        mesh=mesh,
        in_specs=placed,
        out_specs=(
            P("groups", "space", None, None),
            P("groups", None, "space", None, None),
            P("groups", None),
            P("groups"),
        ),
        check_vma=False,
    )
```

profile of v0, /device:TPU:0, one launch (start us, length us, event | category | flops | bytes accessed | tf_op | source)
XLA Modules:
  0.0 149.3 jit_solution(8708772870478701507)
XLA Ops:
  0.6 9.6 %forward_modes.1 = f32[1,32,32,64]{3,2,1,0:T(8,128)} custom-call(f32[32,1,128,256]{3,2,1,0:T(8,128)} %x_ref.3, bf16[256,128]{1,0:T(8,128)(2,1)} %constant.51.clone.tzh, bf16[256,128]{1,0:T(8,128)(2,1)} %constant.52.clone.tzl, bf16[64,128]{1,0:T(8,128)(2,1)} %constant.53.clone.tyh, bf16[64,128]{1,0:T(8,128)(2,1)} %constant.54.clone.tyl), custom_call_target="tpu_custom_call" | custom-call | tf_op jit(solution)/shard_map/forward_modes/pallas_call | solution.py:110
  10.3 1.6 %reshape.80 = f32[1,32,32,2,32]{4,3,2,1,0:T(2,128)S(1)} reshape(f32[1,32,32,64]{3,2,1,0:T(8,128)} %forward_modes.1) | data formatting | bytes 524288 | tf_op jit(solution)/shard_map/reshape | solution.py:244
  13.8 17.2 %all_to_all.56 = f32[16,1,4096]{2,1,0:T(1,128)S(1)} all-to-all(f32[16,1,4096]{2,1,0:T(1,128)S(1)} %reshape.104), channel_id=1, replica_groups=mesh['groups'=2,'space'=16] {'space'}, dimensions={0} | all-to-all | bytes 524288 | tf_op jit(solution)/shard_map/all_to_all | solution.py:246
  31.6 1.2 reduce.11
  35.7 13.8 %fusion.2 = (f32[32,64,32]{1,2,0:T(8,128)S(1)}, f32[32,64,32]{1,2,0:T(8,128)S(1)}, f32[32,64,32]{1,2,0:T(8,128)S(1)}, f32[32,64,32]{1,2,0:T(8,128)S(1)}) fusion(f32[2,32,64,32,32]{2,4,3,1,0:T(8,128)} %param.22, f32[32,64,32]{1,2,0:T(8,128)S(1)} %copy.131, f32[32,64,32]{1,2,0:T(8,128)S(1)} %copy.132), kind=kLoop, calls=%fused_computation.6 | loop fusion | flops 16515072 | bytes 18350080
  51.3 1.3 reshape.106
  52.6 3.7 %all-to-all-start.1 = ((f32[16,1,4096]{2,1,0:T(1,128)}), f32[16,1,4096]{2,1,0:T(1,128)S(1)}, u32[]{:S(2)}, u32[]{:S(2)}) async-start(f32[16,1,4096]{2,1,0:T(1,128)} %reshape.106), calls=%async_computation.1 | async-start | bytes 524288 | tf_op jit(solution)/shard_map/all_to_all | solution.py:270
  56.6 2.6 %broadcast_multiply_fusion = f32[32,8,32,8]{3,2,1,0:T(8,128)} fusion(f32[8,8]{1,0:T(8,128)S(1)} %fusion.12, f32[32,32]{1,0:T(8,128)S(1)} %copy.84), kind=kLoop, calls=%fused_computation.9 | loop fusion | flops 65536 | bytes 266496 | tf_op jit(solution)/shard_map/mul | solution.py:184
  59.2 4.7 %mul.48.wk_ref = f32[256,256]{1,0:T(8,128)} reshape(f32[32,8,32,8]{3,2,1,0:T(8,128)} %broadcast_multiply_fusion) | data formatting | bytes 524288 | tf_op jit(solution)/shard_map/mul | solution.py:184
  63.9 2.3 %all-to-all-done.1 = f32[16,1,4096]{2,1,0:T(1,128)S(1)} async-done(((f32[16,1,4096]{2,1,0:T(1,128)}), f32[16,1,4096]{2,1,0:T(1,128)S(1)}, u32[]{:S(2)}, u32[]{:S(2)}) %all-to-all-start.1) | async-done | bytes 262176 | tf_op jit(solution)/shard_map/all_to_all | solution.py:270
  66.1 1.2 reduce.12
  69.0 1.6 %copy.83 = f32[1,2,32,32,2,32]{5,4,3,2,1,0:T(2,128)S(1)} copy(f32[1,2,32,32,2,32]{5,2,3,4,1,0:T(8,128)S(1)} %pad_maximum_fusion) | data formatting | bytes 1048576 | tf_op jit(solution)/shard_map/stack | solution.py:273
  70.6 3.5 %reshape.83.m_ref = f32[1,64,2048]{2,1,0:T(8,128)} reshape(f32[1,2,32,32,2,32]{5,4,3,2,1,0:T(2,128)S(1)} %copy.83) | data formatting | bytes 1048576 | tf_op jit(solution)/shard_map/reshape | solution.py:274
  74.9 21.5 %middle.1 = (bf16[32,1,128,256]{3,2,1,0:T(8,128)(2,1)}, f32[1,32,32,64]{3,2,1,0:T(8,128)}, f32[1,32,256]{2,1,0:T(8,128)}) custom-call(f32[1,64,2048]{2,1,0:T(8,128)} %reshape.83.m_ref, f32[32,1,128,256]{3,2,1,0:T(8,128)} %x_ref.3, bf16[32,1,128,256]{3,2,1,0:T(8,128)(2,1)} %cot_ref.1, f32[256,256]{1,0:T(8,128)} %mul.48.wk_ref, ...), custom_call_target="tpu_custom_call" | custom-call | tf_op jit(solution)/shard_map/middle/pallas_call | solution.py:188
  99.2 3.7 %all-to-all-start.3 = ((f32[16,1,1056]{2,1,0:T(1,128)}), f32[16,1,1056]{2,1,0:T(1,128)S(1)}, u32[]{:S(2)}, u32[]{:S(2)}) async-start(f32[16,1,1056]{2,1,0:T(1,128)} %reshape.110), calls=%async_computation.3 | async-start | bytes 147456 | tf_op jit(solution)/shard_map/all_to_all | solution.py:292
  102.9 1.7 %reshape.84 = f32[1,32,32,2,32]{4,3,2,1,0:T(2,128)S(1)} reshape(f32[1,32,32,64]{3,2,1,0:T(8,128)} %get-tuple-element.8) | data formatting | bytes 524288 | tf_op jit(solution)/shard_map/reshape | solution.py:244
  105.4 1.8 %reshape.108 = f32[16,1,4096]{2,1,0:T(1,128)} reshape(f32[1024,1,2,32]{3,2,1,0:T(2,128)S(1)} %bitcast.132) | data formatting | bytes 524288
  107.2 2.5 %all-to-all-done.3 = f32[16,1,1056]{2,1,0:T(1,128)S(1)} async-done(((f32[16,1,1056]{2,1,0:T(1,128)}), f32[16,1,1056]{2,1,0:T(1,128)S(1)}, u32[]{:S(2)}, u32[]{:S(2)}) %all-to-all-start.3) | async-done | bytes 67616 | tf_op jit(solution)/shard_map/all_to_all | solution.py:292
  109.7 3.5 %all-to-all-start.2 = ((f32[16,1,4096]{2,1,0:T(1,128)}), f32[16,1,4096]{2,1,0:T(1,128)S(1)}, u32[]{:S(2)}, u32[]{:S(2)}) async-start(f32[16,1,4096]{2,1,0:T(1,128)} %reshape.108), calls=%async_computation.2 | async-start | bytes 524288 | tf_op jit(solution)/shard_map/all_to_all | solution.py:246
  113.3 1.6 %copy.89.s_ref = f32[2,32,32,64]{3,2,1,0:T(8,128)} copy(f32[2,32,32,64]{3,1,2,0:T(8,128)S(1)} %convolution_bitcast_fusion.1) | data formatting | bytes 1048576 | tf_op jit(solution)/shard_map/xrcm,xrqk->qkcm/dot_general | solution.py:250
  117.4 5.8 %all-to-all-done.2 = f32[16,1,4096]{2,1,0:T(1,128)S(1)} async-done(((f32[16,1,4096]{2,1,0:T(1,128)}), f32[16,1,4096]{2,1,0:T(1,128)S(1)}, u32[]{:S(2)}, u32[]{:S(2)}) %all-to-all-start.2) | async-done | bytes 262176 | tf_op jit(solution)/shard_map/all_to_all | solution.py:246
  123.2 1.2 reduce.13
  126.6 1.6 %fusion.6.d_ref = f32[2,32,32,64]{3,2,1,0:T(8,128)} fusion(f32[32,64,2,32]{1,3,2,0:T(8,128)S(1)} %convolution_bitcast_fusion, f32[64]{0:T(128)S(1)} %compare_select_fusion.2), kind=kLoop, calls=%fused_computation.19 | loop fusion | flops 131072 | bytes 1048832 | tf_op jit(solution)/shard_map/mul | solution.py:298
  128.2 21.0 %weight_gradient.1 = f32[2,32,32,32,64]{4,3,2,1,0:T(8,128)} custom-call(f32[2,32,32,64]{3,2,1,0:T(8,128)} %copy.89.s_ref, f32[2,32,32,64]{3,2,1,0:T(8,128)} %fusion.6.d_ref), custom_call_target="tpu_custom_call" | custom-call | tf_op jit(solution)/shard_map/weight_gradient/pallas_call | solution.py:227
  (54 shorter events, 17.9 us)
Async XLA Ops:
  12.0 22.3 %copy-start.2 = (f32[16,2,2,32,1]{3,0,1,4,2:T(8,128)S(1)}, f32[16,2,2,32,1]{3,0,1,4,2:T(8,128)}, u32[]{:S(2)}) copy-start(f32[16,2,2,32,1]{3,0,1,4,2:T(8,128)} %constant.67) | copy-start | bytes 24580
  35.7 15.0 %copy-start.1 = (f32[2,2,16,32,1]{3,2,0,1,4:T(8,128)S(1)}, f32[2,2,16,32,1]{3,2,0,1,4:T(8,128)}, u32[]{:S(2)}) copy-start(f32[2,2,16,32,1]{3,2,0,1,4:T(8,128)} %constant.68) | copy-start | bytes 24580
  49.4 6.9 %copy-start.3 = (f32[32,32]{1,0:T(8,128)S(1)}, f32[32,32]{1,0:T(8,128)}, u32[]{:S(2)}) copy-start(f32[32,32]{1,0:T(8,128)} %param.23) | copy-start | bytes 12292
  49.4 7.0 %copy-start.4 = (f32[32]{0:T(128)S(1)}, f32[32]{0:T(128)}, u32[]{:S(2)}) copy-start(f32[32]{0:T(128)} %param.24) | copy-start | bytes 388
  52.6 13.5 %all-to-all-start.1 = ((f32[16,1,4096]{2,1,0:T(1,128)}), f32[16,1,4096]{2,1,0:T(1,128)S(1)}, u32[]{:S(2)}, u32[]{:S(2)}) async-start(f32[16,1,4096]{2,1,0:T(1,128)} %reshape.106), calls=%async_computation.1 | async-start | bytes 524288 | tf_op jit(solution)/shard_map/all_to_all | solution.py:270
  99.2 10.5 %all-to-all-start.3 = ((f32[16,1,1056]{2,1,0:T(1,128)}), f32[16,1,1056]{2,1,0:T(1,128)S(1)}, u32[]{:S(2)}, u32[]{:S(2)}) async-start(f32[16,1,1056]{2,1,0:T(1,128)} %reshape.110), calls=%async_computation.3 | async-start | bytes 147456 | tf_op jit(solution)/shard_map/all_to_all | solution.py:292
  105.4 20.6 %copy-start = (f32[16,2,2,32,1]{3,0,1,2,4:T(8,128)S(1)}, f32[16,2,2,32,1]{3,0,1,2,4:T(8,128)}, u32[]{:S(2)}) copy-start(f32[16,2,2,32,1]{3,0,1,2,4:T(8,128)} %constant.69) | copy-start | bytes 24580
  109.7 13.5 %all-to-all-start.2 = ((f32[16,1,4096]{2,1,0:T(1,128)}), f32[16,1,4096]{2,1,0:T(1,128)S(1)}, u32[]{:S(2)}, u32[]{:S(2)}) async-start(f32[16,1,4096]{2,1,0:T(1,128)} %reshape.108), calls=%async_computation.2 | async-start | bytes 524288 | tf_op jit(solution)/shard_map/all_to_all | solution.py:246
where the time goes:
time: 152 us; the launch traced here: 149 us
  Pallas kernels  52.1 us (34%)
  local copies, waits for them, and re-layouts  30.5 us (20%)
  other arithmetic  25.1 us (17%)
  blocking collectives  17.2 us (11%)
  starting transfers between devices  11 us (7%)
  waiting for transfers between devices  10.6 us (7%)
  matrix products  1.66 us (1%)
    pallas_call x1, Pallas kernels, middle(): pl.pallas_call(middle_kernel, grid=(width, ny // STEP), out_shape=(jax.Sh...  21.5 us
    pallas_call x1, Pallas kernels, weight_gradient(): pl.pallas_call(gradient_kernel, grid=(kx,), out_shape=jax.ShapeDtypeStruc...  21 us
    all_to_all x1, blocking collectives, to_spectrum(): lax.all_to_all(lines, 'space', split_axis=3, concat_axis=0, tiled=True)  17.2 us
    unnamed x1, other arithmetic  13.8 us
    pallas_call x1, Pallas kernels, forward_modes(): pl.pallas_call(forward_kernel, grid=(width, ny // STEP), out_shape=jax.Sh...  9.63 us
    unnamed x23, local copies, waits for them, and re-layouts  8.87 us
    all_to_all x1, waiting for transfers between devices, to_spectrum(): lax.all_to_all(lines, 'space', split_axis=3, concat_axis=0, tiled=True)  5.83 us
    mul x1, local copies, waits for them, and re-layouts, middle(): point_weights.T[:, None, :, None] * eye[None, :, None, :]  4.66 us
  transfers between devices with their start and end apart: 3, of which 3 were waited for; matrix products, arithmetic and copies ran while one was open for 11% of the time, Pallas kernels for 0%

commit v1 on v0

v1 whole, which is shorter than its diff:
```python
import functools

import jax
import jax.numpy as jnp
import numpy as np
from jax import lax
from jax.experimental import pallas as pl
from jax.experimental.pallas import tpu as pltpu
from jax.sharding import PartitionSpec as P

MX = 32
MY = 32
MZ = 32
ROWS = 8
STEP = 32

HIGH = lax.Precision.HIGH
INV_SQRT_TWO = 0.7071067811865476
INV_SQRT_TWO_PI = 0.3989422804014327


def angles(positions, frequency, length):
    product = np.outer(np.asarray(positions), np.asarray(frequency)) % length
    phase = 2.0 * np.pi / length * product.astype(np.float64)
    return np.cos(phase), np.sin(phase)


def kept(count, length):
    index = np.arange(count)
    return np.where(index < count // 2, index, length - count + index)


def halves(table):
    table = np.asarray(table, np.float32)
    high = table.astype(jnp.bfloat16)
    low = (table - high.astype(np.float32)).astype(jnp.bfloat16)
    return jnp.asarray(high), jnp.asarray(low)


def split(value):
    high = value.astype(jnp.bfloat16)
    low = (value - high.astype(jnp.float32)).astype(jnp.bfloat16)
    return high, low


def dot3(a, b, dims=(((1,), (0,)), ((), ()))):
    one = functools.partial(
        lax.dot_general, dimension_numbers=dims, preferred_element_type=jnp.float32
    )
    return one(a[0], b[0]) + (one(a[0], b[1]) + one(a[1], b[0]))


def forward_tables(ny, nz):
    cos_z, sin_z = angles(np.arange(nz), np.arange(MZ), nz)
    table_z = np.concatenate([cos_z, -sin_z, -sin_z, -cos_z], axis=1)
    cos_y, sin_y = angles(np.arange(ny), kept(MY, ny), ny)
    table_y = np.concatenate([cos_y.T, sin_y.T], axis=0)
    return halves(table_z) + halves(table_y)


def inverse_tables(ny, nz, scale, local_rows):
    cos_z, sin_z = angles(np.arange(nz), np.arange(MZ), nz)
    weight = np.where(np.arange(MZ) == 0, 1.0, 2.0)[:, None] * scale
    real = np.kron(np.eye(4), cos_z.T * weight)
    imag = np.kron(np.eye(4), -sin_z.T * weight)
    cos_y, sin_y = angles(np.arange(ny), kept(MY, ny), ny)
    cos_y = cos_y.reshape(ny, MY // local_rows, local_rows)
    sin_y = sin_y.reshape(ny, MY // local_rows, local_rows)
    real_y = np.stack([cos_y, -sin_y], 2).reshape(ny, 2 * MY)
    imag_y = np.stack([sin_y, cos_y], 2).reshape(ny, 2 * MY)
    return halves(np.concatenate([real, imag], 0)) + halves(np.concatenate([real_y, imag_y], 0))


def finish_y(lines, ty, modes_ref):
    def one(c, carry):
        both = dot3(ty, split(lines[c]))
        turned = pltpu.roll(both[MY:], 2 * MZ, 1)
        modes_ref[c] = (both[:MY] + turned)[:, : 2 * MZ]
        return carry

    lax.fori_loop(0, lines.shape[0], one, 0, unroll=16)


def forward_kernel(x_ref, tzh, tzl, tyh, tyl, modes_ref, lines):
    step = pl.program_id(1)
    channels, rows, nz = x_ref.shape
    value = x_ref[...].reshape(channels * rows, nz)
    along = dot3(split(value), (tzh[...], tzl[...]))
    start = pl.multiple_of(step * rows, rows)
    lines[:, pl.ds(start, rows), :] = along.reshape(channels, rows, 4 * MZ)

    @pl.when(step == pl.num_programs(1) - 1)
    def _():
        finish_y(lines, (tyh[...], tyl[...]), modes_ref)


def whole(array):
    shape = array.shape
    return pl.BlockSpec(shape, lambda *_: (0,) * len(shape))


def field_spec(channels, nz):
    return pl.BlockSpec((channels, None, STEP, nz), lambda x, y: (0, x, y, 0))


def modes_spec(channels):
    return pl.BlockSpec((None, channels, MY, 2 * MZ), lambda x, y: (x, 0, 0, 0))


def forward_modes(field):
    channels, width, ny, nz = field.shape
    tables = forward_tables(ny, nz)
    return pl.pallas_call(
        forward_kernel,
        grid=(width, ny // STEP),
        out_shape=jax.ShapeDtypeStruct((width, channels, MY, 2 * MZ), jnp.float32),
        in_specs=[field_spec(channels, nz)] + [whole(t) for t in tables],
        out_specs=modes_spec(channels),
        scratch_shapes=[pltpu.VMEM((channels, ny, 4 * MZ), jnp.float32)],
        name="forward_modes",
    )(field, *tables)


def middle_kernel(
    m_ref, x_ref, cot_ref, w_ref, bias_ref, pick, bdh, bdl, iyh, iyl, tzh, tzl, tyh, tyl,
    act_ref, modes_ref, point_ref, lines, inverse, field_part, wh, wl, total,
):
    step = pl.program_id(1)
    channels, rows, nz = x_ref.shape
    quads = channels // 4
    width = 4 * MZ
    ny = lines.shape[1]

    def same_row():
        size = channels * ROWS
        row = lax.broadcasted_iota(jnp.int32, (size, size), 0) % ROWS
        column = lax.broadcasted_iota(jnp.int32, (size, size), 1) % ROWS
        return row == column

    @pl.when(step == 0)
    def _():
        for part in range(0, m_ref.shape[1], 256):
            lanes = pl.ds(part, 256)
            both = dot3((iyh[...], iyl[...]), split(m_ref[:, lanes]))
            inverse[0, :, lanes] = both[:ny]
            inverse[1, :, lanes] = both[ny:]
        contract = (((1,), (1,)), ((), ()))
        for narrow, out in zip(split(w_ref[...]), (wh, wl)):
            tall = lax.dot_general(
                pick[...], narrow, contract, preferred_element_type=jnp.float32
            ).astype(jnp.bfloat16)
            square = lax.dot_general(tall, pick[...], contract, preferred_element_type=jnp.float32)
            out[...] = jnp.where(same_row(), square, 0.0).astype(jnp.bfloat16)
        total[...] = jnp.zeros_like(total)

    first = pl.multiple_of(step * rows, rows)
    stacked = jnp.concatenate(
        [
            jnp.concatenate(
                [
                    inverse[r, pl.ds(first, rows), g * width : (g + 1) * width]
                    for r in range(2)
                ],
                axis=1,
            )
            for g in range(quads)
        ],
        axis=0,
    )
    stacked = split(stacked)
    for c in range(4):
        lanes = slice(c * nz, (c + 1) * nz)
        field_part[:, lanes] = dot3(stacked, (bdh[:, lanes], bdl[:, lanes]))

    for half in range(rows // ROWS):
        here = slice(half * ROWS, (half + 1) * ROWS)
        start = pl.multiple_of(step * rows + half * ROWS, ROWS)
        spectral = jnp.concatenate(
            [
                field_part[
                    g * rows + half * ROWS : g * rows + (half + 1) * ROWS, c * nz : (c + 1) * nz
                ]
                for g in range(quads)
                for c in range(4)
            ],
            axis=0,
        )
        field = split(x_ref[:, here, :].reshape(channels * ROWS, nz))
        before = spectral + dot3((wh[...], wl[...]), field)
        before = before.reshape(channels, ROWS, nz) + bias_ref[...]
        normal = 0.5 * (1.0 + lax.erf(before * INV_SQRT_TWO))
        density = jnp.exp(-0.5 * before * before) * INV_SQRT_TWO_PI
        act_ref[:, here, :] = (before * normal).astype(jnp.bfloat16)
        slope = cot_ref[:, here, :].astype(jnp.float32) * (normal + before * density)
        slope = split(slope.reshape(channels * ROWS, nz))
        total[...] += dot3(field, slope, (((1,), (1,)), ((), ())))
        along = dot3(slope, (tzh[...], tzl[...]))
        lines[:, pl.ds(start, ROWS), :] = along.reshape(channels, ROWS, 4 * MZ)

    @pl.when(step == pl.num_programs(1) - 1)
    def _():
        finish_y(lines, (tyh[...], tyl[...]), modes_ref)
        size = channels * ROWS
        diagonal = jnp.where(same_row(), total[...], 0.0)
        point_ref[...] = jnp.sum(diagonal.reshape(channels, ROWS, size), axis=1)


def middle(grid_modes, local_rows, field, cotangent, point_weights, point_bias, scale):
    channels, width, ny, nz = field.shape
    size = channels * ROWS
    tables = inverse_tables(ny, nz, scale, local_rows) + forward_tables(ny, nz)
    pick = jnp.asarray(np.repeat(np.eye(channels, dtype=np.float32), ROWS, 0).astype(jnp.bfloat16))
    bias = jnp.broadcast_to(point_bias[:, None, None], (channels, 1, nz))
    spec = field_spec(channels, nz)
    mixed_spec = pl.BlockSpec((None,) + grid_modes.shape[1:], lambda x, y: (x, 0, 0))
    return pl.pallas_call(
        middle_kernel,
        grid=(width, ny // STEP),
        out_shape=(
            jax.ShapeDtypeStruct(field.shape, jnp.bfloat16),
            jax.ShapeDtypeStruct((width, channels, MY, 2 * MZ), jnp.float32),
            jax.ShapeDtypeStruct((width, channels, size), jnp.float32),
        ),
        in_specs=[mixed_spec, spec, spec, whole(point_weights), whole(bias), whole(pick)]
        + [whole(t) for t in tables],
        out_specs=(
            spec,
            modes_spec(channels),
            pl.BlockSpec((None, channels, size), lambda x, y: (x, 0, 0)),
        ),
        scratch_shapes=[
            pltpu.VMEM((channels, ny, 4 * MZ), jnp.float32),
            pltpu.VMEM((2, ny, channels * MZ), jnp.float32),
            pltpu.VMEM((channels // 4 * STEP, 4 * nz), jnp.float32),
            pltpu.VMEM((size, size), jnp.bfloat16),
            pltpu.VMEM((size, size), jnp.bfloat16),
            pltpu.VMEM((size, size), jnp.float32),
        ],
        name="middle",
    )(grid_modes, field, cotangent, point_weights, bias, pick, *tables)


def weight_gradient(spectrum, slope_modes):
    turned = jnp.stack([slope_modes[1], -slope_modes[0]], axis=0)
    slope_modes, turned = lax.optimization_barrier((slope_modes, turned))
    real = spectrum[0][None, :, :, None, :]
    imag = spectrum[1][None, :, :, None, :]
    out = real * slope_modes[:, :, None] + imag * turned[:, :, None]
    return out.transpose(0, 1, 4, 2, 3)


def x_table(length_x):
    return angles(np.arange(length_x), kept(MX, length_x), length_x)


def exchange(lines):
    return lax.all_to_all(lines, "space", split_axis=0, concat_axis=0, tiled=True)


def to_spectrum(modes, scale, devices, extra=None):
    width, channels = modes.shape[:2]
    local = MY * MZ // devices
    lines = modes.reshape(width, channels, MY, 2, MZ).transpose(0, 3, 1, 2, 4)
    lines = lines.reshape(width, 2, channels, devices, local).transpose(3, 0, 1, 2, 4)
    lines = lines.reshape(devices, width * 2 * channels * local)
    size = lines.shape[1]
    if extra is not None:
        extra = jnp.pad(extra, (0, -extra.shape[0] % 128))
        extra = jnp.broadcast_to(extra[None], (devices,) + extra.shape)
        lines = jnp.concatenate([lines, extra], axis=1)
    lines = exchange(lines)
    summed = jnp.sum(lines[:, size:], axis=0)
    lines = lines[:, :size].reshape(devices * width, 2, channels, local)
    cos_x, sin_x = x_table(devices * width)
    table = np.stack([np.stack([cos_x, -sin_x], 1), np.stack([sin_x, cos_x], 1)], 1)
    table = jnp.asarray((table * scale).astype(np.float32))
    return jnp.einsum("xrcm,xrqk->qkcm", lines, table, precision=HIGH), summed


def mix_modes(spectrum, weights):
    real, imag = spectrum[0], spectrum[1]
    out_real = jnp.einsum("kim,kmio->kom", real, weights[0], precision=HIGH) - jnp.einsum(
        "kim,kmio->kom", imag, weights[1], precision=HIGH
    )
    out_imag = jnp.einsum("kim,kmio->kom", real, weights[1], precision=HIGH) + jnp.einsum(
        "kim,kmio->kom", imag, weights[0], precision=HIGH
    )
    return jnp.stack([out_real, out_imag], axis=0)


def to_grid(mixed, length_x):
    channels = mixed.shape[2]
    cos_x, sin_x = x_table(length_x)
    table = np.stack([np.stack([cos_x, sin_x], 0), np.stack([-sin_x, cos_x], 0)], 0)
    table = jnp.asarray(table.astype(np.float32))
    lines = jnp.einsum("rkom,rqxk->xqom", mixed, table, precision=HIGH)
    local = mixed.shape[3]
    devices = MY * MZ // local
    width = length_x // devices
    if local % MZ == 0:
        local_rows = local // MZ
        lines = lines.reshape(length_x, 2, channels, local_rows, MZ).transpose(0, 1, 3, 2, 4)
        lines = exchange(lines.reshape(length_x, 2 * local_rows * channels * MZ))
        grid = lines.reshape(devices, width, 2 * local_rows, channels * MZ).transpose(1, 0, 2, 3)
    else:
        local_rows = 1
        lines = exchange(lines.reshape(length_x, 2 * channels * local))
        grid = lines.reshape(MY, MZ // local, width, 2, channels, local).transpose(2, 0, 3, 4, 1, 5)
    return grid.reshape(width, 2 * MY, channels * MZ), local_rows


def body(lifted_field, cotangent, spectral_weights, point_weights, point_bias):
    devices = lax.axis_size("space")
    channels, width, ny, nz = lifted_field.shape
    length_x = width * devices
    scale = 1.0 / float(length_x * ny * nz) ** 0.5
    spectrum, _ = to_spectrum(forward_modes(lifted_field), scale, devices)
    grid_modes, local_rows = to_grid(mix_modes(spectrum, spectral_weights), length_x)
    activated, slope_modes, wide_point = middle(
        grid_modes, local_rows, lifted_field, cotangent, point_weights, point_bias, scale
    )
    local_point = jnp.sum(wide_point.reshape(width, channels, channels, ROWS), axis=(0, 3))
    local_bias = jnp.sum(slope_modes[:, :, 0, 0], axis=0)
    partial = jnp.concatenate([local_point.reshape(-1), local_bias])
    slope_spectrum, summed = to_spectrum(slope_modes, scale, devices, partial)
    area = channels * channels
    summed_point = summed[:area].reshape(channels, channels)
    summed_bias = summed[area : area + channels]
    local_modes = spectrum.shape[3]
    mode_ids = lax.axis_index("space") * local_modes + jnp.arange(local_modes, dtype=jnp.int32)
    weight_modes = jnp.where(mode_ids % MZ == 0, 1.0, 2.0).astype(jnp.float32)
    grad_spectral = weight_gradient(spectrum, slope_spectrum * weight_modes)
    return (activated, grad_spectral, summed_point * scale, summed_bias * scale)


def solution(mesh):
    placed = (
        P("groups", "space", None, None),
        P("groups", "space", None, None),
        P(None, None, "space", None, None),
        P(),
        P(),
    )
    return jax.shard_map(
        body,
        mesh=mesh,
        in_specs=placed,
        out_specs=(
            P("groups", "space", None, None),
            P("groups", None, "space", None, None),
            P("groups", None),
            P("groups"),
        ),
        check_vma=False,
    )
```

time: 152 us -> 116 us (0.76); the launches traced: 149 us -> 115 us
  Pallas kernels: 52.1 us -> 24.3 us
  local copies, waits for them, and re-layouts: 30.5 us -> 14.4 us
  blocking collectives: 17.2 us -> 29.9 us
  starting transfers between devices: 11 us -> 3.54 us
  other arithmetic: 25.1 us -> 28.3 us
    pallas_call x1 -> x0, Pallas kernels: 21 us -> none  [weight_gradient(): pl.pallas_call(gradient_kernel, grid=(kx,), out_shape=jax.ShapeDtypeStruc...]
    all_to_all x1 -> x2, blocking collectives: 17.2 us -> 29.9 us  [exchange(): lax.all_to_all(lines, 'space', split_axis=0, concat_axis=0, tiled=True)]
    add x0 -> x1, other arithmetic: none -> 11.6 us  [weight_gradient(): out = real * slope_modes[:, :, None] + imag * turned[:, :, None]]
    unnamed x23 -> x10, local copies, waits for them, and re-layouts: 8.87 us -> 0.73 us
    all_to_all x3 -> x1, starting transfers between devices: 11 us -> 3.54 us  [exchange(): lax.all_to_all(lines, 'space', split_axis=0, concat_axis=0, tiled=True)]
    mul x4 -> x2, other arithmetic: 4.96 us -> 0.52 us  [body(): return (activated, grad_spectral, summed_point * scale, summed_bias * scale)]
    pallas_call x1, Pallas kernels: 21.5 us -> 17.9 us  [middle(): pl.pallas_call(middle_kernel, grid=(width, ny // STEP), out_shape=(jax.Sh...]
    reshape x4 -> x7, local copies, waits for them, and re-layouts: 5.03 us -> 1.72 us  [the longest x1 0.61 us: to_grid(): lines.reshape(length_x, 2, channels, local_rows, MZ)]
  transfers between devices with their start and end apart: 3 -> 1, of which waited for: 3 -> 1; matrix products, arithmetic and copies ran while one was open for 11% -> 0% of each run, Pallas kernels for 0% -> 0%
where the time goes in v1:
time: 116 us; the launch traced here: 115 us
  blocking collectives  29.9 us (26%)
  other arithmetic  28.3 us (24%)
  Pallas kernels  24.3 us (21%)
  local copies, waits for them, and re-layouts  14.4 us (12%)
  waiting for transfers between devices  11.1 us (10%)
  starting transfers between devices  3.54 us (3%)
  matrix products  2.83 us (2%)
    all_to_all x2, blocking collectives, exchange(): lax.all_to_all(lines, 'space', split_axis=0, concat_axis=0, tiled=True)  29.9 us
    pallas_call x1, Pallas kernels, middle(): pl.pallas_call(middle_kernel, grid=(width, ny // STEP), out_shape=(jax.Sh...  17.9 us
    unnamed x1, other arithmetic  13.5 us
    add x1, other arithmetic, weight_gradient(): out = real * slope_modes[:, :, None] + imag * turned[:, :, None]  11.6 us
    all_to_all x1, waiting for transfers between devices, exchange(): lax.all_to_all(lines, 'space', split_axis=0, concat_axis=0, tiled=True)  11.1 us
    pallas_call x1, Pallas kernels, forward_modes(): pl.pallas_call(forward_kernel, grid=(width, ny // STEP), out_shape=jax.Sh...  6.41 us
    reshape x4, local copies, waits for them, and re-layouts, to_spectrum(): lines = modes.reshape(width, channels, MY, 2, MZ).transpose(0, 3, 1, 2, 4)  3.56 us
    all_to_all x1, starting transfers between devices, exchange(): lax.all_to_all(lines, 'space', split_axis=0, concat_axis=0, tiled=True)  3.54 us
  transfers between devices with their start and end apart: 1, of which 1 were waited for; matrix products, arithmetic and copies ran while one was open for 0% of the time, Pallas kernels for 0%

profile of v1, /device:TPU:0, one launch (start us, length us, event | category | flops | bytes accessed | tf_op | source)
XLA Modules:
  0.0 115.4 jit_solution(6096809287507132110)
XLA Ops:
  0.6 6.4 %forward_modes.1 = f32[1,32,32,64]{3,2,1,0:T(8,128)} custom-call(f32[32,1,128,256]{3,2,1,0:T(8,128)} %x_ref.3, bf16[256,128]{1,0:T(8,128)(2,1)} %constant.55.clone.tzh, bf16[256,128]{1,0:T(8,128)(2,1)} %constant.56.clone.tzl, bf16[64,128]{1,0:T(8,128)(2,1)} %constant.57.clone.tyh, bf16[64,128]{1,0:T(8,128)(2,1)} %constant.58.clone.tyl), custom_call_target="tpu_custom_call" | custom-call | tf_op jit(solution)/shard_map/forward_modes/pallas_call | solution.py:113
  7.0 1.6 %reshape.89 = f32[1,32,32,2,32]{4,3,2,1,0:T(2,128)S(1)} reshape(f32[1,32,32,64]{3,2,1,0:T(8,128)} %forward_modes.1) | data formatting | bytes 524288 | tf_op jit(solution)/shard_map/reshape | solution.py:263
  9.6 17.2 %all_to_all.31 = f32[16,1,4096]{2,1,0:T(1,128)S(1)} all-to-all(f32[16,1,4096]{2,1,0:T(1,128)S(1)} %all_to_all.27), channel_id=1, replica_groups=mesh['groups'=2,'space'=16] {'space'}, dimensions={0} | all-to-all | bytes 524288 | tf_op jit(solution)/shard_map/all_to_all | solution.py:257
  26.8 0.6 reduce.5
  27.6 1.6 %convolution_bitcast_fusion.1 = f32[2,32,32,64]{3,1,2,0:T(8,128)S(1)} fusion(f32[16,2,2,32,1]{3,0,1,4,2:T(8,128)} %constant.74, f32[16,2,32,64]{3,2,1,0:T(8,128)S(1)} %reshape.91), kind=kOutput, calls=%fused_computation.10 | convolution fusion | flops 25165824 | bytes 794624 | tf_op jit(solution)/shard_map/xrcm,xrqk->qkcm/dot_general | solution.py:277
  29.9 13.5 %fusion.2 = (f32[32,64,32]{1,2,0:T(8,128)S(1)}, f32[32,64,32]{1,2,0:T(8,128)S(1)}, f32[32,64,32]{1,2,0:T(8,128)S(1)}, f32[32,64,32]{1,2,0:T(8,128)S(1)}) fusion(f32[2,32,64,32,32]{2,4,3,1,0:T(8,128)} %param.23, f32[32,64,32]{1,2,0:T(8,128)S(1)} %copy.108, f32[32,64,32]{1,2,0:T(8,128)S(1)} %copy.109), kind=kLoop, calls=%fused_computation.7 | loop fusion | flops 16515072 | bytes 18350080
  43.4 1.2 fusion.10
  45.6 0.6 copy.60
  46.7 12.7 %all_to_all.32 = f32[16,1,4096]{2,1,0:T(1,128)S(1)} all-to-all(f32[16,1,4096]{2,1,0:T(1,128)S(1)} %all_to_all.22), channel_id=1, replica_groups=mesh['groups'=2,'space'=16] {'space'}, dimensions={0} | all-to-all | bytes 524288 | tf_op jit(solution)/shard_map/all_to_all | solution.py:257
  59.4 0.6 reduce.6
  60.0 0.8 reshape_transpose_reshape.3.m_ref
  60.8 0.7 broadcast_in_dim.12.bias_ref
  61.5 17.9 %middle.1 = (bf16[32,1,128,256]{3,2,1,0:T(8,128)(2,1)}, f32[1,32,32,64]{3,2,1,0:T(8,128)}, f32[1,32,256]{2,1,0:T(8,128)}) custom-call(f32[1,64,1024]{2,1,0:T(8,128)} %reshape_transpose_reshape.3.m_ref, f32[32,1,128,256]{3,2,1,0:T(8,128)} %x_ref.3, bf16[32,1,128,256]{3,2,1,0:T(8,128)(2,1)} %cot_ref.1, f32[32,32]{1,0:T(8,128)} %w_ref.1, ...), custom_call_target="tpu_custom_call" | custom-call | tf_op jit(solution)/shard_map/middle/pallas_call | solution.py:216
  79.5 1.2 %slice_reduce_fusion.1 = f32[32]{0:T(128)S(1)} fusion(f32[1,32,32,64]{3,2,1,0:T(8,128)} %get-tuple-element.10), kind=kLoop, calls=%fused_computation.34 | loop fusion | bytes 256 | tf_op jit(solution)/shard_map/slice | solution.py:323
  80.7 1.6 %reshape.93 = f32[1,32,32,2,32]{4,3,2,1,0:T(2,128)S(1)} reshape(f32[1,32,32,64]{3,2,1,0:T(8,128)} %get-tuple-element.10) | data formatting | bytes 524288 | tf_op jit(solution)/shard_map/reshape | solution.py:263
  82.3 0.9 copy.64
  84.2 1.1 copy.66
  85.2 3.5 %all-to-all-start.2 = ((f32[16,1,5248]{2,1,0:T(1,128)}), f32[16,1,5248]{2,1,0:T(1,128)S(1)}, u32[]{:S(2)}, u32[]{:S(2)}) async-start(f32[16,1,5248]{2,1,0:T(1,128)} %copy.66), calls=%async_computation.2 | async-start | bytes 671744 | tf_op jit(solution)/shard_map/all_to_all | solution.py:257
  88.8 11.1 %all-to-all-done.2 = f32[16,1,5248]{2,1,0:T(1,128)S(1)} async-done(((f32[16,1,5248]{2,1,0:T(1,128)}), f32[16,1,5248]{2,1,0:T(1,128)S(1)}, u32[]{:S(2)}, u32[]{:S(2)}) %all-to-all-start.2) | async-done | bytes 335904 | tf_op jit(solution)/shard_map/all_to_all | solution.py:257
  100.6 0.7 mul.81
  101.5 0.8 fusion.5
  102.5 0.6 copy.68
  103.1 0.6 copy.70
  103.8 11.6 %multiply_add_fusion = f32[2,32,64,32,32]{2,4,3,1,0:T(8,128)} fusion(f32[2,32,64,32]{2,3,1,0:T(8,128)S(1)} %copy.70, f32[32,64,32]{1,2,0:T(8,128)S(1)} %copy.109, f32[2,32,64,32]{2,3,1,0:T(8,128)S(1)} %copy.68, f32[32,64,32]{1,2,0:T(8,128)S(1)} %copy.108), kind=kLoop, calls=%fused_computation | loop fusion | flops 12582912 | bytes 18350080 | tf_op jit(solution)/shard_map/add | solution.py:248
  (36 shorter events, 5.2 us)
Async XLA Ops:
  29.9 14.7 %copy-start.1 = (f32[2,2,16,32,1]{3,2,0,1,4:T(8,128)S(1)}, f32[2,2,16,32,1]{3,2,0,1,4:T(8,128)}, u32[]{:S(2)}) copy-start(f32[2,2,16,32,1]{3,2,0,1,4:T(8,128)} %constant.75) | copy-start | bytes 24580
  29.9 30.9 %copy-start.2 = (f32[32]{0:T(128)S(1)}, f32[32]{0:T(128)}, u32[]{:S(2)}) copy-start(f32[32]{0:T(128)} %param.25) | copy-start | bytes 388
  43.4 58.0 %copy-start = (f32[16,2,2,32,1]{3,0,1,2,4:T(8,128)S(1)}, f32[16,2,2,32,1]{3,0,1,2,4:T(8,128)}, u32[]{:S(2)}) copy-start(f32[16,2,2,32,1]{3,0,1,2,4:T(8,128)} %constant.76) | copy-start | bytes 24580
  85.2 14.7 %all-to-all-start.2 = ((f32[16,1,5248]{2,1,0:T(1,128)}), f32[16,1,5248]{2,1,0:T(1,128)S(1)}, u32[]{:S(2)}, u32[]{:S(2)}) async-start(f32[16,1,5248]{2,1,0:T(1,128)} %copy.66), calls=%async_computation.2 | async-start | bytes 671744 | tf_op jit(solution)/shard_map/all_to_all | solution.py:257

commit v2 on v1

--- a/solution.py
+++ b/solution.py
@@ -253,8 +253,66 @@
     return angles(np.arange(length_x), kept(MX, length_x), length_x)
 
 
-def exchange(lines):
-    return lax.all_to_all(lines, "space", split_axis=0, concat_axis=0, tiled=True)
+def exchange_kernel(devices, src, out, send_sem, recv_sem, own_sem):
+    me = lax.axis_index("space")
+    barrier = pltpu.get_barrier_semaphore()
+
+    def greet(step, carry):
+        peer = lax.rem(me + step, devices)
+        pl.semaphore_signal(
+            barrier, inc=1, device_id={"space": peer}, device_id_type=pl.DeviceIdType.MESH
+        )
+        return carry
+
+    def copy(step, slot):
+        peer = lax.rem(me + step, devices)
+        return pltpu.make_async_remote_copy(
+            src_ref=src.at[peer],
+            dst_ref=out.at[slot],
+            send_sem=send_sem.at[step],
+            recv_sem=recv_sem.at[step],
+            device_id={"space": peer},
+            device_id_type=pl.DeviceIdType.MESH,
+        )
+
+    def send(step, carry):
+        copy(step, me).start()
+        return carry
+
+    def finish(step, carry):
+        done = copy(step, lax.rem(me + devices - step, devices))
+        done.wait_send()
+        done.wait_recv()
+        return carry
+
+    lax.fori_loop(1, devices, greet, 0)
+    own = pltpu.make_async_copy(src.at[me], out.at[me], own_sem)
+    own.start()
+    pl.semaphore_wait(barrier, devices - 1)
+    lax.fori_loop(1, devices, send, 0)
+    own.wait()
+    lax.fori_loop(1, devices, finish, 0)
+
+
+def exchange(lines, identity):
+    devices = lax.axis_size("space")
+    shape = lines.shape
+    lines = lines.reshape(devices, -1, 128)
+    vmem = pl.BlockSpec(memory_space=pltpu.VMEM)
+    out = pl.pallas_call(
+        functools.partial(exchange_kernel, devices),
+        out_shape=jax.ShapeDtypeStruct(lines.shape, jnp.float32),
+        in_specs=[vmem],
+        out_specs=vmem,
+        scratch_shapes=[
+            pltpu.SemaphoreType.DMA((devices,)),
+            pltpu.SemaphoreType.DMA((devices,)),
+            pltpu.SemaphoreType.DMA,
+        ],
+        compiler_params=pltpu.CompilerParams(collective_id=identity, has_side_effects=True),
+        name=f"exchange_{identity}",
+    )(lines)
+    return out.reshape(shape)
 
 
 def to_spectrum(modes, scale, devices, extra=None):
@@ -268,7 +326,7 @@
         extra = jnp.pad(extra, (0, -extra.shape[0] % 128))
         extra = jnp.broadcast_to(extra[None], (devices,) + extra.shape)
         lines = jnp.concatenate([lines, extra], axis=1)
-    lines = exchange(lines)
+    lines = exchange(lines, 0 if extra is None else 2)
     summed = jnp.sum(lines[:, size:], axis=0)
     lines = lines[:, :size].reshape(devices * width, 2, channels, local)
     cos_x, sin_x = x_table(devices * width)
@@ -300,11 +358,11 @@
     if local % MZ == 0:
         local_rows = local // MZ
         lines = lines.reshape(length_x, 2, channels, local_rows, MZ).transpose(0, 1, 3, 2, 4)
-        lines = exchange(lines.reshape(length_x, 2 * local_rows * channels * MZ))
+        lines = exchange(lines.reshape(length_x, 2 * local_rows * channels * MZ), 1)
         grid = lines.reshape(devices, width, 2 * local_rows, channels * MZ).transpose(1, 0, 2, 3)
     else:
         local_rows = 1
-        lines = exchange(lines.reshape(length_x, 2 * channels * local))
+        lines = exchange(lines.reshape(length_x, 2 * channels * local), 1)
         grid = lines.reshape(MY, MZ // local, width, 2, channels, local).transpose(2, 0, 3, 4, 1, 5)
     return grid.reshape(width, 2 * MY, channels * MZ), local_rows
 

time: 116 us -> 113 us (0.974)
  Pallas kernels: 24.3 us -> 62.8 us
  blocking collectives: 29.9 us -> 0 us
  waiting for transfers between devices: 11.1 us -> 0 us
  local copies, waits for them, and re-layouts: 14.4 us -> 18.7 us
  starting transfers between devices: 3.54 us -> 0 us
  other arithmetic: 28.3 us -> 27.1 us
    pallas_call x0 -> x3, Pallas kernels: none -> 38.4 us  [exchange(): pl.pallas_call(functools.partial(exchange_kernel, devices), out_shape=jax...]
    all_to_all x2 -> x0, blocking collectives: 29.9 us -> none  [exchange(): lax.all_to_all(lines, 'space', split_axis=0, concat_axis=0, tiled=True)]
    all_to_all x1 -> x0, waiting for transfers between devices: 11.1 us -> none  [exchange(): lax.all_to_all(lines, 'space', split_axis=0, concat_axis=0, tiled=True)]
    all_to_all x1 -> x0, starting transfers between devices: 3.54 us -> none  [exchange(): lax.all_to_all(lines, 'space', split_axis=0, concat_axis=0, tiled=True)]
    another operation x0 -> x3, local copies, waits for them, and re-layouts: none -> 2.92 us  [the longest x2 1.82 us: exchange(): lines = lines.reshape(devices, -1, 128)]
    all_to_all x3 -> x0, local copies, waits for them, and re-layouts: 1.85 us -> none  [exchange(): lax.all_to_all(lines, 'space', split_axis=0, concat_axis=0, tiled=True)]
    all_to_all x3 -> x0, other arithmetic: 1.26 us -> none  [exchange(): lax.all_to_all(lines, 'space', split_axis=0, concat_axis=0, tiled=True)]
  transfers between devices with their start and end apart: 1 -> 0, of which waited for: 1 -> 0; matrix products, arithmetic and copies ran while one was open for 0% -> 0% of each run, Pallas kernels for 0% -> 0%
where the time goes in v2:
time: 113 us; the launch traced here: 112 us
  Pallas kernels  62.8 us (56%)
  other arithmetic  27.1 us (24%)
  local copies, waits for them, and re-layouts  18.7 us (17%)
  matrix products  2.83 us (3%)
    pallas_call x3, Pallas kernels, exchange(): pl.pallas_call(functools.partial(exchange_kernel, devices), out_shape=jax...  38.4 us
    pallas_call x1, Pallas kernels, middle(): pl.pallas_call(middle_kernel, grid=(width, ny // STEP), out_shape=(jax.Sh...  18.1 us
    unnamed x1, other arithmetic  13.5 us
    add x1, other arithmetic, weight_gradient(): out = real * slope_modes[:, :, None] + imag * turned[:, :, None]  11.6 us
    pallas_call x1, Pallas kernels, forward_modes(): pl.pallas_call(forward_kernel, grid=(width, ny // STEP), out_shape=jax.Sh...  6.38 us
    reshape x4, local copies, waits for them, and re-layouts, to_spectrum(): lines = modes.reshape(width, channels, MY, 2, MZ).transpose(0, 3, 1, 2, 4)  3.56 us
    dot_general x2, matrix products, to_spectrum(): return (jnp.einsum('xrcm,xrqk->qkcm', lines, table, precision=HIGH), summed)  2.4 us

profile of v2, /device:TPU:0, one launch (start us, length us, event | category | flops | bytes accessed | tf_op | source)
XLA Modules:
  0.0 112.3 jit_solution(2982345556036741848)
XLA Ops:
  0.7 1.4 %broadcast_in_dim.12.bias_ref = f32[32,1,256]{2,1,0:T(1,128)} broadcast(f32[32]{0:T(128)} %param.25), dimensions={0} | broadcast | bytes 32896 | tf_op jit(solution)/shard_map/broadcast_in_dim | solution.py:213
  2.0 6.4 %forward_modes.1 = f32[1,32,32,64]{3,2,1,0:T(8,128)} custom-call(f32[32,1,128,256]{3,2,1,0:T(8,128)} %x_ref.3, bf16[256,128]{1,0:T(8,128)(2,1)} %constant.55.clone.tzh, bf16[256,128]{1,0:T(8,128)(2,1)} %constant.56.clone.tzl, bf16[64,128]{1,0:T(8,128)(2,1)} %constant.57.clone.tyh, bf16[64,128]{1,0:T(8,128)(2,1)} %constant.58.clone.tyl), custom_call_target="tpu_custom_call" | custom-call | tf_op jit(solution)/shard_map/forward_modes/pallas_call | solution.py:113
  8.4 1.6 %reshape.80 = f32[1,32,32,2,32]{4,3,2,1,0:T(2,128)S(1)} reshape(f32[1,32,32,64]{3,2,1,0:T(8,128)} %forward_modes.1) | data formatting | bytes 524288 | tf_op jit(solution)/shard_map/reshape | solution.py:321
  10.6 0.8 reshape_reshape.9.src
  11.4 12.7 %exchange_0.1 = f32[16,32,128]{2,1,0:T(8,128)} custom-call(f32[16,32,128]{2,1,0:T(8,128)} %reshape_reshape.9.src), custom_call_target="tpu_custom_call" | custom-call | tf_op jit(solution)/shard_map/exchange_0/pallas_call | solution.py:302
  24.2 1.1 reshape_reshape.10
  25.3 1.6 %convolution_bitcast_fusion.1 = f32[2,32,32,64]{3,1,2,0:T(8,128)S(1)} fusion(f32[16,2,2,32,1]{3,0,1,4,2:T(8,128)} %constant.74, f32[16,2,32,64]{3,2,1,0:T(8,128)S(1)} %reshape_reshape.10), kind=kOutput, calls=%fused_computation.10 | convolution fusion | flops 25165824 | bytes 794624 | tf_op jit(solution)/shard_map/xrcm,xrqk->qkcm/dot_general | solution.py:335
  27.6 13.5 %fusion.2 = (f32[32,64,32]{1,2,0:T(8,128)S(1)}, f32[32,64,32]{1,2,0:T(8,128)S(1)}, f32[32,64,32]{1,2,0:T(8,128)S(1)}, f32[32,64,32]{1,2,0:T(8,128)S(1)}) fusion(f32[2,32,64,32,32]{2,4,3,1,0:T(8,128)} %param.23, f32[32,64,32]{1,2,0:T(8,128)S(1)} %copy.115, f32[32,64,32]{1,2,0:T(8,128)S(1)} %copy.116), kind=kLoop, calls=%fused_computation.7 | loop fusion | flops 16515072 | bytes 18350080
  41.1 1.2 %fusion.10 = (f32[1,32,32,64]{3,1,0,2:T(8,128)S(1)}, f32[1,32,32,64]{3,1,0,2:T(8,128)S(1)}) fusion(f32[32,64,32]{1,2,0:T(8,128)S(1)} %get-tuple-element.18, f32[32,64,32]{1,2,0:T(8,128)S(1)} %get-tuple-element.15, f32[32,64,32]{1,2,0:T(8,128)S(1)} %get-tuple-element.19, f32[32,64,32]{1,2,0:T(8,128)S(1)} %get-tuple-element.14), kind=kLoop, calls=%fused_computation.27 | loop fusion | flops 131072 | bytes 1572864 | tf_op jit(solution)/shard_map/stack | solution.py:346
  43.3 0.6 copy.139
  43.9 1.0 reshape_reshape.11.src
  44.9 12.2 %exchange_1.1 = f32[16,32,128]{2,1,0:T(8,128)} custom-call(f32[16,32,128]{2,1,0:T(8,128)} %reshape_reshape.11.src), custom_call_target="tpu_custom_call" | custom-call | tf_op jit(solution)/shard_map/exchange_1/pallas_call | solution.py:302
  57.1 1.7 %reshape_transpose_reshape_reshape.3.m_ref = f32[1,64,1024]{2,1,0:T(8,128)} reshape(f32[16,32,128]{2,1,0:T(8,128)} %exchange_1.1) | data formatting | bytes 524288 | tf_op jit(solution)/shard_map/reshape;transpose;reshape;reshape | solution.py:367
  58.8 18.1 %middle.1 = (bf16[32,1,128,256]{3,2,1,0:T(8,128)(2,1)}, f32[1,32,32,64]{3,2,1,0:T(8,128)}, f32[1,32,256]{2,1,0:T(8,128)}) custom-call(f32[1,64,1024]{2,1,0:T(8,128)} %reshape_transpose_reshape_reshape.3.m_ref, f32[32,1,128,256]{3,2,1,0:T(8,128)} %x_ref.3, bf16[32,1,128,256]{3,2,1,0:T(8,128)(2,1)} %cot_ref.1, f32[32,32]{1,0:T(8,128)} %w_ref.1, ...), custom_call_target="tpu_custom_call" | custom-call | tf_op jit(solution)/shard_map/middle/pallas_call | solution.py:216
  76.8 1.2 %slice_reduce_fusion.1 = f32[32]{0:T(128)S(1)} fusion(f32[1,32,32,64]{3,2,1,0:T(8,128)} %get-tuple-element.10), kind=kLoop, calls=%fused_computation.35 | loop fusion | bytes 256 | tf_op jit(solution)/shard_map/slice | solution.py:381
  78.1 0.9 copy.73
  79.1 1.7 %reshape.83 = f32[1,32,32,2,32]{4,3,2,1,0:T(2,128)S(1)} reshape(f32[1,32,32,64]{3,2,1,0:T(8,128)} %get-tuple-element.10) | data formatting | bytes 524288 | tf_op jit(solution)/shard_map/reshape | solution.py:321
  81.6 0.8 reshape.88.src
  82.4 13.5 %exchange_2.1 = f32[16,41,128]{2,1,0:T(8,128)} custom-call(f32[16,41,128]{2,1,0:T(8,128)} %reshape.88.src), custom_call_target="tpu_custom_call" | custom-call | tf_op jit(solution)/shard_map/exchange_2/pallas_call | solution.py:302
  95.8 1.1 copy.141
  97.5 0.7 mul.81
  98.4 0.8 fusion.5
  99.5 0.6 copy.76
  100.7 11.6 %multiply_add_fusion = f32[2,32,64,32,32]{2,4,3,1,0:T(8,128)} fusion(f32[2,32,64,32]{2,3,1,0:T(8,128)S(1)} %copy.78, f32[32,64,32]{1,2,0:T(8,128)S(1)} %copy.116, f32[2,32,64,32]{2,3,1,0:T(8,128)S(1)} %copy.76, f32[32,64,32]{1,2,0:T(8,128)S(1)} %copy.115), kind=kLoop, calls=%fused_computation | loop fusion | flops 12582912 | bytes 18350080 | tf_op jit(solution)/shard_map/add | solution.py:248
  (31 shorter events, 4.8 us)
Async XLA Ops:
  27.6 14.7 %copy-start.1 = (f32[2,2,16,32,1]{3,2,0,1,4:T(8,128)S(1)}, f32[2,2,16,32,1]{3,2,0,1,4:T(8,128)}, u32[]{:S(2)}) copy-start(f32[2,2,16,32,1]{3,2,0,1,4:T(8,128)} %constant.75) | copy-start | bytes 24580
  41.1 57.3 %copy-start = (f32[16,2,2,32,1]{3,0,1,2,4:T(8,128)S(1)}, f32[16,2,2,32,1]{3,0,1,2,4:T(8,128)}, u32[]{:S(2)}) copy-start(f32[16,2,2,32,1]{3,0,1,2,4:T(8,128)} %constant.76) | copy-start | bytes 24580
